TPU v7x, 512 devices: a whole 4x8x8 slice. The times are simulated.
512 devices in a mesh: row: 16 (over y, core), col: 32 (over z, x).
Axes of the slice: x: 4, y: 8, z: 8, core: 2. Of those that a mesh axis runs over, the one named last changes fastest.
Arguments:
- surface: float32 [2, 1024, 4096], P(None, 'row', 'col'), may hold values from -0.5 to 0.5
- u_face: float32 [2, 1024, 4096], P(None, 'row', 'col'), may hold values from -3 to 3
- v_face: float32 [2, 1024, 4096], P(None, 'row', 'col'), may hold values from -3 to 3
- bed_depth: float32 [1024, 4096], P('row', 'col'), may hold values from 1 to 10
- wet_mask: int32 [2, 1024, 4096], P(None, 'row', 'col'), may hold values 0 or 1
- rainfall: float32 [2, 1024, 4096], P(None, 'row', 'col'), may hold values from 0.05 to 0.5
Outputs:
- new_surface: float32 [2, 1024, 4096], P(None, 'row', 'col')
- new_u: float32 [2, 1024, 4096], P(None, 'row', 'col')
- new_v: float32 [2, 1024, 4096], P(None, 'row', 'col')
All inputs are finite; a program needn't handle non-finite values. No bound on the sum of `wet_mask` on one device may be relied on, other than what follows from the above.
Results may differ from a plain program's by a relative error of at most 0.0003.
Values sent between devices are 32-bit elements; how exact they have to be, the bound alone decides.
A program may use at most 64 MiB of HBM per device.

v0:
```python
import jax
import jax.numpy as jnp
from jax import lax
from jax.sharding import PartitionSpec as P

ITERS = 3
DTDX = 0.5
FRIC = 0.05
G1 = 4.0
CK = DTDX * G1


def extended(cells, sides, width):
    for axis, dim in sides:
        count = lax.axis_size(axis)
        ends = count - 1
        head = lax.slice_in_dim(cells, 0, width, axis=dim)
        tail = lax.slice_in_dim(cells, cells.shape[dim] - width, cells.shape[dim], axis=dim)
        cells = jnp.concatenate(
            [
                lax.ppermute(tail, axis, [(i, (i + 1) % count) for i in range(ends)]),
                cells,
                lax.ppermute(head, axis, [((i + 1) % count, i) for i in range(ends)]),
            ],
            axis=dim,
        )
    return cells


def passed_along(block, axis, distance):
    devices = range(lax.axis_size(axis))
    route = [(i - distance, i) for i in devices if i - distance in devices]
    return lax.ppermute(block, axis, route)


def explicit(eta2, u2, v2, dep2, wet2, ny, nx):

    def view(a, dy, dx):
        return a[:, 1 + dy : 3 + dy + ny, 1 + dx : 3 + dx + nx]

    h_here = view(eta2, 0, 0) + view(dep2, 0, 0)
    h_east = view(eta2, 0, 1) + view(dep2, 0, 1)
    h_north = view(eta2, 1, 0) + view(dep2, 1, 0)
    wet_x = view(wet2, 0, 0) * view(wet2, 0, 1)
    wet_y = view(wet2, 0, 0) * view(wet2, 1, 0)
    depth_x = 0.5 * (h_here + h_east)
    depth_y = 0.5 * (h_here + h_north)
    u_here = view(u2, 0, 0)
    v_here = view(v2, 0, 0)
    v_mean = 0.25 * (v_here + view(v2, 0, 1) + view(v2, -1, 0) + view(v2, -1, 1))
    u_mean = 0.25 * (u_here + view(u2, 0, -1) + view(u2, 1, 0) + view(u2, 1, -1))
    adv_u = jnp.where(
        u_here > 0, u_here * (u_here - view(u2, 0, -1)), u_here * (view(u2, 0, 1) - u_here)
    )
    adv_u = adv_u + jnp.where(
        v_mean > 0, v_mean * (u_here - view(u2, -1, 0)), v_mean * (view(u2, 1, 0) - u_here)
    )
    adv_v = jnp.where(
        v_here > 0, v_here * (v_here - view(v2, -1, 0)), v_here * (view(v2, 1, 0) - v_here)
    )
    adv_v = adv_v + jnp.where(
        u_mean > 0, u_mean * (v_here - view(v2, 0, -1)), u_mean * (view(v2, 0, 1) - v_here)
    )
    u_star = wet_x * (u_here - DTDX * adv_u) / (1.0 + FRIC * jnp.abs(u_here))
    v_star = wet_y * (v_here - DTDX * adv_v) / (1.0 + FRIC * jnp.abs(v_here))
    return (
        u_star,
        v_star,
        wet_x,
        wet_y,
        CK * depth_x * wet_x,
        CK * depth_y * wet_y,
        depth_x * u_star,
        depth_y * v_star,
    )


def inner(a):
    return a[:, 1:-1, 1:-1]


def right_side(eta, rain, flux_x, flux_y):
    div = inner(flux_x) - flux_x[:, 1:-1, :-2] + (inner(flux_y) - flux_y[:, :-2, 1:-1])
    return eta + rain - DTDX * div


def operate(e_pad, coef_x, coef_y):
    e_mid = inner(e_pad)
    out = (
        e_mid
        + inner(coef_x) * (e_mid - e_pad[:, 1:-1, 2:])
        + coef_x[:, 1:-1, :-2] * (e_mid - e_pad[:, 1:-1, :-2])
    )
    return (
        out
        + inner(coef_y) * (e_mid - e_pad[:, 2:, 1:-1])
        + coef_y[:, :-2, 1:-1] * (e_mid - e_pad[:, :-2, 1:-1])
    )


def field_pad(field):
    return extended(field, (("row", 1), ("col", 2)), 1)


def squares(residual):
    return lax.psum(jnp.sum(residual * residual, axis=(1, 2)), ("row", "col"))


def spread(values):
    return values[:, None, None]


def body(surface, u_face, v_face, bed_depth, wet_mask, rainfall):
    rows = surface.shape[1]
    cols = surface.shape[2]
    stacked = jnp.stack(
        [
            surface,
            u_face,
            v_face,
            jnp.broadcast_to(bed_depth[None], surface.shape),
            wet_mask.astype(jnp.float32),
        ]
    )
    padded = extended(stacked, (("row", 2), ("col", 3)), 2)
    u_star, v_star, wet_x, wet_y, coef_x, coef_y, flux_x, flux_y = explicit(
        padded[0], padded[1], padded[2], padded[3], padded[4], rows, cols
    )
    rhs = right_side(surface, rainfall, flux_x, flux_y)
    start_pad = padded[0][:, 1:-1, 1:-1]
    solution = surface
    residual = rhs - operate(start_pad, coef_x, coef_y)
    direction = residual
    norm_now = squares(residual)
    for step in range(ITERS):
        direction_pad = field_pad(direction)
        image = operate(direction_pad, coef_x, coef_y)
        alpha = norm_now / lax.psum(jnp.sum(direction * image, axis=(1, 2)), ("row", "col"))
        solution = solution + spread(alpha) * direction
        residual = residual - spread(alpha) * image
        norm_next = squares(residual)
        direction = residual + spread(norm_next / norm_now) * direction
        norm_now = norm_next
    east_col = passed_along(solution[:, :, :1], "col", -1)
    north_row = passed_along(solution[:, :1, :], "row", -1)
    east_field = jnp.concatenate([solution[:, :, 1:], east_col], axis=2)
    north_field = jnp.concatenate([solution[:, 1:, :], north_row], axis=1)
    new_u = inner(u_star) - G1 * inner(wet_x) * (east_field - solution)
    new_v = inner(v_star) - G1 * inner(wet_y) * (north_field - solution)
    return (solution, new_u, new_v)


def solution(mesh):
    in_specs = (
        P(None, "row", "col"),
        P(None, "row", "col"),
        P(None, "row", "col"),
        P("row", "col"),
        P(None, "row", "col"),
        P(None, "row", "col"),
    )
    out_specs = (P(None, "row", "col"), P(None, "row", "col"), P(None, "row", "col"))
    return jax.shard_map(body, mesh=mesh, in_specs=in_specs, out_specs=out_specs, check_vma=False)
```

profile of v0, /device:TPU:14, one launch (start us, length us, event | category | flops | bytes accessed | tf_op | source)
XLA Modules:
  0.0 589.8 jit_solution(1745346275453686401)
XLA Ops:
  4.0 1.9 collective-permute-start
  5.9 3.6 collective-permute-start.1
  11.1 4.2 collective-permute-start.2
  15.3 1.9 collective-permute-start.3
  17.3 6.6 %collective-permute-done.2 = f32[5,2,68,2]{3,2,1,0:T(8,128)S(1)} collective-permute-done((f32[5,2,68,2]{3,2,1,0:T(8,128)S(1)}, f32[5,2,68,2]{3,2,1,0:T(8,128)S(1)}, u32[]{:S(2)}, u32[]{:S(2)}) %collective-permute-start.2) | collective-permute-done | bytes 5472 | tf_op jit(solution)/shard_map/ppermute | solution.py:21
  23.8 6.6 %collective-permute-done.3 = f32[5,2,68,2]{3,2,1,0:T(8,128)S(1)} collective-permute-done((f32[5,2,68,2]{3,2,1,0:T(8,128)S(1)}, f32[5,2,68,2]{3,2,1,0:T(8,128)S(1)}, u32[]{:S(2)}, u32[]{:S(2)}) %collective-permute-start.3) | collective-permute-done | bytes 5472 | tf_op jit(solution)/shard_map/ppermute | solution.py:23
  32.9 1.9 collective-permute-start.5
  34.8 2.4 collective-permute-start.4
  37.3 2.5 collective-permute-done.4
  39.8 1.9 collective-permute-start.6
  41.7 6.0 %collective-permute-start.7 = (f32[2,66,1]{2,1,0:T(8,128)S(1)}, f32[2,66,1]{2,1,0:T(8,128)S(1)}, u32[]{:S(2)}, u32[]{:S(2)}) collective-permute-start(f32[2,66,1]{2,1,0:T(8,128)S(1)} %get-tuple-element.39), channel_id=1, source_target_pairs={{0,1},{1,2},{2,3},{3,4},{4,5},{5,6},{6,7},{7,8},{8,9},{9,10},{10,1... | collective-permute-start | bytes 1592 | tf_op jit(solution)/shard_map/ppermute | solution.py:21
  48.2 1.6 collective-permute-done.7
  50.0 105.9 %all-reduce = (f32[2]{0:T(128)S(1)}, f32[2]{0:T(128)S(1)}) all-reduce(f32[2]{0:T(128)S(1)} %get-tuple-element.4, f32[2]{0:T(128)S(1)} %get-tuple-element.3), channel_id=1, replica_groups=mesh['row'=16,'col'=32] {'row','col'}, use_global_device_ids=true, to_apply=%region_1.2 | all-reduce | flops 4 | bytes 32 | tf_op jit(solution)/shard_map/psum | solution.py:106
  156.1 94.5 %psum.44 = f32[2]{0:T(128)S(1)} all-reduce(f32[2]{0:T(128)S(1)} %get-tuple-element.9), channel_id=1, replica_groups=mesh['row'=16,'col'=32] {'row','col'}, use_global_device_ids=true, to_apply=%region_5.6 | all-reduce | flops 2 | bytes 16 | tf_op jit(solution)/shard_map/psum | solution.py:106
  250.7 1.9 collective-permute-start.9
  252.6 2.4 collective-permute-start.8
  255.1 2.5 collective-permute-done.8
  257.6 2.2 collective-permute-start.10
  259.8 5.8 collective-permute-start.11
  266.0 1.6 collective-permute-done.11
  267.8 99.5 %psum.45 = f32[2]{0:T(128)S(1)} all-reduce(f32[2]{0:T(128)S(1)} %get-tuple-element.7), channel_id=1, replica_groups=mesh['row'=16,'col'=32] {'row','col'}, use_global_device_ids=true, to_apply=%region_7.8 | all-reduce | flops 2 | bytes 16 | tf_op jit(solution)/shard_map/psum | solution.py:138
  367.5 94.4 %psum.46 = f32[2]{0:T(128)S(1)} all-reduce(f32[2]{0:T(128)S(1)} %multiply_reduce_fusion), channel_id=1, replica_groups=mesh['row'=16,'col'=32] {'row','col'}, use_global_device_ids=true, to_apply=%region_9.10 | all-reduce | flops 2 | bytes 16 | tf_op jit(solution)/shard_map/psum | solution.py:106
  461.9 1.9 collective-permute-start.13
  463.9 2.4 collective-permute-start.12
  466.3 2.5 collective-permute-done.12
  468.8 2.2 collective-permute-start.14
  471.1 5.7 collective-permute-start.15
  477.2 1.6 collective-permute-done.15
  479.0 99.4 %psum.47 = f32[2]{0:T(128)S(1)} all-reduce(f32[2]{0:T(128)S(1)} %fusion.28), channel_id=1, replica_groups=mesh['row'=16,'col'=32] {'row','col'}, use_global_device_ids=true, to_apply=%region_11.12 | all-reduce | flops 2 | bytes 16 | tf_op jit(solution)/shard_map/psum | solution.py:138
  578.5 1.9 collective-permute-start.17
  580.5 1.9 collective-permute-start.16
  582.5 6.5 %collective-permute-done.16 = f32[2,64,1]{2,1,0:T(8,128)S(1)} collective-permute-done((f32[2,64,1]{2,1,0:T(8,128)S(1)}, f32[2,64,1]{2,1,0:T(8,128)S(1)}, u32[]{:S(2)}, u32[]{:S(2)}) %collective-permute-start.16) | collective-permute-done | bytes 544 | tf_op jit(solution)/shard_map/ppermute | solution.py:33
  (63 shorter events, 11.0 us)
Async XLA Ops:
  0.6 0.9 copy-start.3
  1.5 0.8 copy-start.4
  2.4 0.8 copy-start.6
  3.1 0.8 copy-start.5
  4.0 5.6 collective-permute-start
  5.9 5.0 collective-permute-start.1
  11.1 12.7 %collective-permute-start.2 = (f32[5,2,68,2]{3,2,1,0:T(8,128)S(1)}, f32[5,2,68,2]{3,2,1,0:T(8,128)S(1)}, u32[]{:S(2)}, u32[]{:S(2)}) collective-permute-start(f32[5,2,68,2]{3,2,1,0:T(8,128)S(1)} %get-tuple-element.30), channel_id=1, source_target_pairs={{0,1},{1,2},{2,3},{3,4},{4,5},{5,6},{6,7},{7,8},{8,9},{9,10},{10,1... | collective-permute-start | bytes 16328 | tf_op jit(solution)/shard_map/ppermute | solution.py:21
  15.3 15.1 %collective-permute-start.3 = (f32[5,2,68,2]{3,2,1,0:T(8,128)S(1)}, f32[5,2,68,2]{3,2,1,0:T(8,128)S(1)}, u32[]{:S(2)}, u32[]{:S(2)}) collective-permute-start(f32[5,2,68,2]{3,2,1,0:T(8,128)S(1)} %get-tuple-element.31), channel_id=1, source_target_pairs={{1,0},{2,1},{3,2},{4,3},{5,4},{6,5},{7,6},{8,7},{9,8},{10,9},{11,1... | collective-permute-start | bytes 16328 | tf_op jit(solution)/shard_map/ppermute | solution.py:23
  31.8 0.8 copy-start.1
  31.8 0.9 copy-start.2
  32.9 4.3 collective-permute-start.5
  34.8 4.9 collective-permute-start.4
  39.8 8.4 %collective-permute-start.6 = (f32[2,66,1]{2,1,0:T(8,128)S(1)}, f32[2,66,1]{2,1,0:T(8,128)S(1)}, u32[]{:S(2)}, u32[]{:S(2)}) collective-permute-start(f32[2,66,1]{2,1,0:T(8,128)S(1)} %get-tuple-element.38), channel_id=1, source_target_pairs={{1,0},{2,1},{3,2},{4,3},{5,4},{6,5},{7,6},{8,7},{9,8},{10,9},{11,1... | collective-permute-start | bytes 1592 | tf_op jit(solution)/shard_map/ppermute | solution.py:23
  41.7 8.0 %collective-permute-start.7 = (f32[2,66,1]{2,1,0:T(8,128)S(1)}, f32[2,66,1]{2,1,0:T(8,128)S(1)}, u32[]{:S(2)}, u32[]{:S(2)}) collective-permute-start(f32[2,66,1]{2,1,0:T(8,128)S(1)} %get-tuple-element.39), channel_id=1, source_target_pairs={{0,1},{1,2},{2,3},{3,4},{4,5},{5,6},{6,7},{7,8},{8,9},{9,10},{10,1... | collective-permute-start | bytes 1592 | tf_op jit(solution)/shard_map/ppermute | solution.py:21
  250.7 4.3 collective-permute-start.9
  252.6 4.9 collective-permute-start.8
  257.6 8.4 %collective-permute-start.10 = (f32[2,66,1]{2,1,0:T(8,128)S(1)}, f32[2,66,1]{2,1,0:T(8,128)S(1)}, u32[]{:S(2)}, u32[]{:S(2)}) collective-permute-start(f32[2,66,1]{2,1,0:T(8,128)S(1)} %get-tuple-element.36), channel_id=1, source_target_pairs={{1,0},{2,1},{3,2},{4,3},{5,4},{6,5},{7,6},{8,7},{9,8},{10,9},{11,1... | collective-permute-start | bytes 1592 | tf_op jit(solution)/shard_map/ppermute | solution.py:23
  259.8 7.7 %collective-permute-start.11 = (f32[2,66,1]{2,1,0:T(8,128)S(1)}, f32[2,66,1]{2,1,0:T(8,128)S(1)}, u32[]{:S(2)}, u32[]{:S(2)}) collective-permute-start(f32[2,66,1]{2,1,0:T(8,128)S(1)} %get-tuple-element.37), channel_id=1, source_target_pairs={{0,1},{1,2},{2,3},{3,4},{4,5},{5,6},{6,7},{7,8},{8,9},{9,10},{10,1... | collective-permute-start | bytes 1592 | tf_op jit(solution)/shard_map/ppermute | solution.py:21
  461.9 4.3 collective-permute-start.13
  463.9 4.9 collective-permute-start.12
  468.8 8.4 %collective-permute-start.14 = (f32[2,66,1]{2,1,0:T(8,128)S(1)}, f32[2,66,1]{2,1,0:T(8,128)S(1)}, u32[]{:S(2)}, u32[]{:S(2)}) collective-permute-start(f32[2,66,1]{2,1,0:T(8,128)S(1)} %get-tuple-element.34), channel_id=1, source_target_pairs={{1,0},{2,1},{3,2},{4,3},{5,4},{6,5},{7,6},{8,7},{9,8},{10,9},{11,1... | collective-permute-start | bytes 1592 | tf_op jit(solution)/shard_map/ppermute | solution.py:23
  471.1 7.7 %collective-permute-start.15 = (f32[2,66,1]{2,1,0:T(8,128)S(1)}, f32[2,66,1]{2,1,0:T(8,128)S(1)}, u32[]{:S(2)}, u32[]{:S(2)}) collective-permute-start(f32[2,66,1]{2,1,0:T(8,128)S(1)} %get-tuple-element.35), channel_id=1, source_target_pairs={{0,1},{1,2},{2,3},{3,4},{4,5},{5,6},{6,7},{7,8},{8,9},{9,10},{10,1... | collective-permute-start | bytes 1592 | tf_op jit(solution)/shard_map/ppermute | solution.py:21
  578.5 10.5 %copy-start = (f32[2,64,128]{2,1,0:T(8,128)}, f32[2,64,128]{2,1,0:T(8,128)S(1)}, u32[]{:S(2)}) copy-start(f32[2,64,128]{2,1,0:T(8,128)S(1)} %multiply_add_fusion) | copy-start | bytes 196612
  578.5 10.4 %collective-permute-start.17 = (f32[2,1,128]{2,1,0:T(1,128)S(1)}, f32[2,1,128]{2,1,0:T(1,128)S(1)}, u32[]{:S(2)}, u32[]{:S(2)}) collective-permute-start(f32[2,1,128]{2,1,0:T(1,128)S(1)} %slice.398), channel_id=1, source_target_pairs={{32,0},{64,32},{96,64},{128,96},{160,128},{192,160},{224,192},{256... | collective-permute-start | bytes 3080 | tf_op jit(solution)/shard_map/ppermute | solution.py:33
  580.5 8.5 %collective-permute-start.16 = (f32[2,64,1]{2,1,0:T(8,128)S(1)}, f32[2,64,1]{2,1,0:T(8,128)S(1)}, u32[]{:S(2)}, u32[]{:S(2)}) collective-permute-start(f32[2,64,1]{2,1,0:T(8,128)S(1)} %bitcast.19), channel_id=1, source_target_pairs={{1,0},{2,1},{3,2},{4,3},{5,4},{6,5},{7,6},{8,7},{9,8},{10,9},{11,1... | collective-permute-start | bytes 1544 | tf_op jit(solution)/shard_map/ppermute | solution.py:33
where the time goes:
time: 591 us; the launch traced here: 590 us
  blocking collectives  494 us (84%)
  starting transfers between devices  52.3 us (9%)
  waiting for transfers between devices  34.3 us (6%)
    psum x3, blocking collectives, squares(): return lax.psum(jnp.sum(residual * residual, axis=(1, 2)), ('row', 'col'))  295 us
    psum x2, blocking collectives, body(): lax.psum(jnp.sum(direction * image, axis=(1, 2)), ('row', 'col'))  199 us
    ppermute x8, starting transfers between devices, extended(): lax.ppermute(tail, axis, [(i, (i + 1) % count) for i in range(ends)])  30.9 us
    ppermute x8, waiting for transfers between devices, extended(): lax.ppermute(tail, axis, [(i, (i + 1) % count) for i in range(ends)])  18.7 us
    ppermute x8, starting transfers between devices, extended(): lax.ppermute(head, axis, [((i + 1) % count, i) for i in range(ends)])  17.6 us
  transfers between devices with their start and end apart: 18, of which 13 were waited for; matrix products, arithmetic and copies ran while one was open for 0% of the time, Pallas kernels for 0%

commit v1 on v0

--- a/solution.py
+++ b/solution.py
@@ -8,6 +8,10 @@
 FRIC = 0.05
 G1 = 4.0
 CK = DTDX * G1
+
+
+def hold_words(my_tile, dev_axis):
+    return jax.lax.all_gather(my_tile, axis_name=dev_axis).sum(axis=0)
 
 
 def extended(cells, sides, width):
@@ -103,7 +107,7 @@
 
 
 def squares(residual):
-    return lax.psum(jnp.sum(residual * residual, axis=(1, 2)), ("row", "col"))
+    return hold_words(jnp.sum(residual * residual, axis=(1, 2)), ("row", "col"))
 
 
 def spread(values):

time: 591 us -> 596 us (level)
    unnamed x0 -> x3, blocking collectives: none -> 295 us
    psum x3 -> x0, blocking collectives: 295 us -> none  [squares(): return lax.psum(jnp.sum(residual * residual, axis=(1, 2)), ('row', 'col'))]
    ppermute x8, waiting for transfers between devices: 18.7 us -> 10.7 us  [extended(): lax.ppermute(tail, axis, [(i, (i + 1) % count) for i in range(ends)])]
where the time goes in v1:
time: 596 us; the launch traced here: 595 us
  blocking collectives  496 us (83%)
  starting transfers between devices  56.1 us (9%)
  waiting for transfers between devices  31.4 us (5%)
    unnamed x3, blocking collectives  295 us
    psum x2, blocking collectives, body(): lax.psum(jnp.sum(direction * image, axis=(1, 2)), ('row', 'col'))  201 us
    ppermute x8, starting transfers between devices, extended(): lax.ppermute(tail, axis, [(i, (i + 1) % count) for i in range(ends)])  29.6 us
    ppermute x8, starting transfers between devices, extended(): lax.ppermute(head, axis, [((i + 1) % count, i) for i in range(ends)])  22.6 us
    ppermute x8, waiting for transfers between devices, extended(): lax.ppermute(head, axis, [((i + 1) % count, i) for i in range(ends)])  14.2 us
  transfers between devices with their start and end apart: 18, of which 13 were waited for; matrix products, arithmetic and copies ran while one was open for 0% of the time, Pallas kernels for 0%

profile of v1, /device:TPU:14, one launch (start us, length us, event | category | flops | bytes accessed | tf_op | source)
XLA Modules:
  0.0 594.7 jit_solution(16830307145957073988)
XLA Ops:
  4.0 1.9 collective-permute-start
  5.9 3.6 collective-permute-start.1
  9.6 1.4 collective-permute-done.1
  11.1 4.2 collective-permute-start.2
  15.3 1.9 collective-permute-start.3
  17.3 6.6 %collective-permute-done.2 = f32[5,2,68,2]{3,2,1,0:T(8,128)S(1)} collective-permute-done((f32[5,2,68,2]{3,2,1,0:T(8,128)S(1)}, f32[5,2,68,2]{3,2,1,0:T(8,128)S(1)}, u32[]{:S(2)}, u32[]{:S(2)}) %collective-permute-start.2) | collective-permute-done | bytes 5472 | tf_op jit(solution)/shard_map/ppermute | solution.py:25
  23.8 6.6 %collective-permute-done.3 = f32[5,2,68,2]{3,2,1,0:T(8,128)S(1)} collective-permute-done((f32[5,2,68,2]{3,2,1,0:T(8,128)S(1)}, f32[5,2,68,2]{3,2,1,0:T(8,128)S(1)}, u32[]{:S(2)}, u32[]{:S(2)}) %collective-permute-start.3) | collective-permute-done | bytes 5472 | tf_op jit(solution)/shard_map/ppermute | solution.py:27
  32.9 2.1 collective-permute-start.4
  35.0 3.5 collective-permute-start.5
  38.5 1.3 collective-permute-done.5
  39.9 1.9 collective-permute-start.6
  41.8 6.0 %collective-permute-start.7 = (f32[2,66,1]{2,1,0:T(8,128)S(1)}, f32[2,66,1]{2,1,0:T(8,128)S(1)}, u32[]{:S(2)}, u32[]{:S(2)}) collective-permute-start(f32[2,66,1]{2,1,0:T(8,128)S(1)} %get-tuple-element.39), channel_id=1, source_target_pairs={{0,1},{1,2},{2,3},{3,4},{4,5},{5,6},{6,7},{7,8},{8,9},{9,10},{10,1... | collective-permute-start | bytes 1592 | tf_op jit(solution)/shard_map/ppermute | solution.py:25
  48.4 1.8 collective-permute-done.7
  50.7 106.2 %all-reduce.3 = (f32[1024]{0:T(1024)S(1)}, f32[2]{0:T(128)S(1)}) all-reduce(f32[1024]{0:T(1024)S(1)} %dynamic-update-slice, f32[2]{0:T(128)S(1)} %get-tuple-element.3), channel_id=2, replica_groups=mesh['row'=16,'col'=32] {'row','col'}, use_global_device_ids=true, to_apply=%add | all-reduce | flops 1026 | bytes 8208
  157.5 94.5 %all-reduce.1 = f32[1024]{0:T(1024)S(1)} all-reduce(f32[1024]{0:T(1024)S(1)} %dynamic-update-slice.1), channel_id=3, replica_groups=mesh['row'=16,'col'=32] {'row','col'}, use_global_device_ids=true, to_apply=%add.1 | all-reduce | flops 1024 | bytes 8192
  252.4 1.9 collective-permute-start.8
  254.3 3.6 collective-permute-start.9
  258.0 1.3 collective-permute-done.9
  259.3 2.2 collective-permute-start.10
  261.5 5.8 collective-permute-start.11
  268.3 1.2 collective-permute-done.11
  269.8 100.5 %psum.22 = f32[2]{0:T(128)S(1)} all-reduce(f32[2]{0:T(128)S(1)} %get-tuple-element.7), channel_id=1, replica_groups=mesh['row'=16,'col'=32] {'row','col'}, use_global_device_ids=true, to_apply=%region_7.8 | all-reduce | flops 2 | bytes 16 | tf_op jit(solution)/shard_map/psum | solution.py:142
  370.6 94.5 %all-reduce.2 = f32[1024]{0:T(1024)S(1)} all-reduce(f32[1024]{0:T(1024)S(1)} %dynamic-update-slice.2), channel_id=4, replica_groups=mesh['row'=16,'col'=32] {'row','col'}, use_global_device_ids=true, to_apply=%add.2 | all-reduce | flops 1024 | bytes 8192
  465.5 1.9 collective-permute-start.12
  467.4 3.6 collective-permute-start.13
  471.0 1.3 collective-permute-done.13
  472.4 2.2 collective-permute-start.14
  474.6 5.8 collective-permute-start.15
  482.7 100.6 %psum.23 = f32[2]{0:T(128)S(1)} all-reduce(f32[2]{0:T(128)S(1)} %fusion.28), channel_id=1, replica_groups=mesh['row'=16,'col'=32] {'row','col'}, use_global_device_ids=true, to_apply=%region_11.12 | all-reduce | flops 2 | bytes 16 | tf_op jit(solution)/shard_map/psum | solution.py:142
  583.4 1.9 collective-permute-start.17
  585.3 1.9 collective-permute-start.16
  587.4 6.5 %collective-permute-done.16 = f32[2,64,1]{2,1,0:T(8,128)S(1)} collective-permute-done((f32[2,64,1]{2,1,0:T(8,128)S(1)}, f32[2,64,1]{2,1,0:T(8,128)S(1)}, u32[]{:S(2)}, u32[]{:S(2)}) %collective-permute-start.16) | collective-permute-done | bytes 544 | tf_op jit(solution)/shard_map/ppermute | solution.py:37
  (75 shorter events, 13.6 us)
Async XLA Ops:
  0.6 0.9 copy-start.3
  1.5 0.8 copy-start.4
  2.4 0.8 copy-start.6
  3.1 0.8 copy-start.5
  4.0 5.6 collective-permute-start
  5.9 5.0 collective-permute-start.1
  11.1 12.7 %collective-permute-start.2 = (f32[5,2,68,2]{3,2,1,0:T(8,128)S(1)}, f32[5,2,68,2]{3,2,1,0:T(8,128)S(1)}, u32[]{:S(2)}, u32[]{:S(2)}) collective-permute-start(f32[5,2,68,2]{3,2,1,0:T(8,128)S(1)} %get-tuple-element.30), channel_id=1, source_target_pairs={{0,1},{1,2},{2,3},{3,4},{4,5},{5,6},{6,7},{7,8},{8,9},{9,10},{10,1... | collective-permute-start | bytes 16328 | tf_op jit(solution)/shard_map/ppermute | solution.py:25
  15.3 15.1 %collective-permute-start.3 = (f32[5,2,68,2]{3,2,1,0:T(8,128)S(1)}, f32[5,2,68,2]{3,2,1,0:T(8,128)S(1)}, u32[]{:S(2)}, u32[]{:S(2)}) collective-permute-start(f32[5,2,68,2]{3,2,1,0:T(8,128)S(1)} %get-tuple-element.31), channel_id=1, source_target_pairs={{1,0},{2,1},{3,2},{4,3},{5,4},{6,5},{7,6},{8,7},{9,8},{10,9},{11,1... | collective-permute-start | bytes 16328 | tf_op jit(solution)/shard_map/ppermute | solution.py:27
  31.8 0.8 copy-start.1
  31.8 0.9 copy-start.2
  32.9 5.6 collective-permute-start.4
  35.0 4.8 collective-permute-start.5
  39.9 8.5 %collective-permute-start.6 = (f32[2,66,1]{2,1,0:T(8,128)S(1)}, f32[2,66,1]{2,1,0:T(8,128)S(1)}, u32[]{:S(2)}, u32[]{:S(2)}) collective-permute-start(f32[2,66,1]{2,1,0:T(8,128)S(1)} %get-tuple-element.38), channel_id=1, source_target_pairs={{1,0},{2,1},{3,2},{4,3},{5,4},{6,5},{7,6},{8,7},{9,8},{10,9},{11,1... | collective-permute-start | bytes 1592 | tf_op jit(solution)/shard_map/ppermute | solution.py:27
  41.8 8.4 %collective-permute-start.7 = (f32[2,66,1]{2,1,0:T(8,128)S(1)}, f32[2,66,1]{2,1,0:T(8,128)S(1)}, u32[]{:S(2)}, u32[]{:S(2)}) collective-permute-start(f32[2,66,1]{2,1,0:T(8,128)S(1)} %get-tuple-element.39), channel_id=1, source_target_pairs={{0,1},{1,2},{2,3},{3,4},{4,5},{5,6},{6,7},{7,8},{8,9},{9,10},{10,1... | collective-permute-start | bytes 1592 | tf_op jit(solution)/shard_map/ppermute | solution.py:25
  252.4 5.6 collective-permute-start.8
  254.3 4.9 collective-permute-start.9
  259.3 9.0 %collective-permute-start.10 = (f32[2,66,1]{2,1,0:T(8,128)S(1)}, f32[2,66,1]{2,1,0:T(8,128)S(1)}, u32[]{:S(2)}, u32[]{:S(2)}) collective-permute-start(f32[2,66,1]{2,1,0:T(8,128)S(1)} %get-tuple-element.36), channel_id=1, source_target_pairs={{1,0},{2,1},{3,2},{4,3},{5,4},{6,5},{7,6},{8,7},{9,8},{10,9},{11,1... | collective-permute-start | bytes 1592 | tf_op jit(solution)/shard_map/ppermute | solution.py:27
  261.5 8.0 %collective-permute-start.11 = (f32[2,66,1]{2,1,0:T(8,128)S(1)}, f32[2,66,1]{2,1,0:T(8,128)S(1)}, u32[]{:S(2)}, u32[]{:S(2)}) collective-permute-start(f32[2,66,1]{2,1,0:T(8,128)S(1)} %get-tuple-element.37), channel_id=1, source_target_pairs={{0,1},{1,2},{2,3},{3,4},{4,5},{5,6},{6,7},{7,8},{8,9},{9,10},{10,1... | collective-permute-start | bytes 1592 | tf_op jit(solution)/shard_map/ppermute | solution.py:25
  465.5 5.6 collective-permute-start.12
  467.4 4.9 collective-permute-start.13
  472.4 8.8 %collective-permute-start.14 = (f32[2,66,1]{2,1,0:T(8,128)S(1)}, f32[2,66,1]{2,1,0:T(8,128)S(1)}, u32[]{:S(2)}, u32[]{:S(2)}) collective-permute-start(f32[2,66,1]{2,1,0:T(8,128)S(1)} %get-tuple-element.34), channel_id=1, source_target_pairs={{1,0},{2,1},{3,2},{4,3},{5,4},{6,5},{7,6},{8,7},{9,8},{10,9},{11,1... | collective-permute-start | bytes 1592 | tf_op jit(solution)/shard_map/ppermute | solution.py:27
  474.6 7.8 %collective-permute-start.15 = (f32[2,66,1]{2,1,0:T(8,128)S(1)}, f32[2,66,1]{2,1,0:T(8,128)S(1)}, u32[]{:S(2)}, u32[]{:S(2)}) collective-permute-start(f32[2,66,1]{2,1,0:T(8,128)S(1)} %get-tuple-element.35), channel_id=1, source_target_pairs={{0,1},{1,2},{2,3},{3,4},{4,5},{5,6},{6,7},{7,8},{8,9},{9,10},{10,1... | collective-permute-start | bytes 1592 | tf_op jit(solution)/shard_map/ppermute | solution.py:25
  583.4 10.5 %copy-start = (f32[2,64,128]{2,1,0:T(8,128)}, f32[2,64,128]{2,1,0:T(8,128)S(1)}, u32[]{:S(2)}) copy-start(f32[2,64,128]{2,1,0:T(8,128)S(1)} %multiply_add_fusion) | copy-start | bytes 196612
  583.4 10.4 %collective-permute-start.17 = (f32[2,1,128]{2,1,0:T(1,128)S(1)}, f32[2,1,128]{2,1,0:T(1,128)S(1)}, u32[]{:S(2)}, u32[]{:S(2)}) collective-permute-start(f32[2,1,128]{2,1,0:T(1,128)S(1)} %slice.398), channel_id=1, source_target_pairs={{32,0},{64,32},{96,64},{128,96},{160,128},{192,160},{224,192},{256... | collective-permute-start | bytes 3080 | tf_op jit(solution)/shard_map/ppermute | solution.py:37
  585.3 8.5 %collective-permute-start.16 = (f32[2,64,1]{2,1,0:T(8,128)S(1)}, f32[2,64,1]{2,1,0:T(8,128)S(1)}, u32[]{:S(2)}, u32[]{:S(2)}) collective-permute-start(f32[2,64,1]{2,1,0:T(8,128)S(1)} %bitcast.19), channel_id=1, source_target_pairs={{1,0},{2,1},{3,2},{4,3},{5,4},{6,5},{7,6},{8,7},{9,8},{10,9},{11,1... | collective-permute-start | bytes 1544 | tf_op jit(solution)/shard_map/ppermute | solution.py:37
